TPU v7x, 128 devices: a whole 4x4x4 slice. The times are simulated.
128 devices in a mesh: dp: 16 (over x_lo, y, core), tensor: 8 (over x_hi, z).
Axes of the slice: x: 4 (x_hi: 2, x_lo: 2; x = x_hi * 2 + x_lo), y: 4, z: 4, core: 2. Of those that a mesh axis runs over, the one named last changes fastest.
Arguments:
- block_input: bfloat16 [32768, 768], P(('dp', 'tensor')), may hold values from -6 to 6
- w_value: bfloat16 [768, 768], replicated, may hold values from -0.21875 to 0.21875
- b_value: bfloat16 [768], replicated, may hold values from -2 to 2
- conv_kernel: bfloat16 [65, 768], replicated, may hold values from -0.75 to 0.75
- w_out: bfloat16 [768, 768], replicated, may hold values from -0.21875 to 0.21875
- b_out: bfloat16 [768], replicated, may hold values from -2 to 2
- gain_attn: bfloat16 [768], replicated, may hold values from 0.5 to 1.5
- shift_attn: bfloat16 [768], replicated, may hold values from -2 to 2
- w_up: bfloat16 [768, 3072], P(None, 'tensor'), may hold values from -0.21875 to 0.21875
- b_up: bfloat16 [3072], P('tensor'), may hold values from -2 to 2
- w_down: bfloat16 [3072, 768], P('tensor'), may hold values from -0.109375 to 0.109375
- b_down: bfloat16 [768], replicated, may hold values from -2 to 2
- gain_ffn: bfloat16 [768], replicated, may hold values from 0.5 to 1.5
- shift_ffn: bfloat16 [768], replicated, may hold values from -2 to 2
- query_codes: int32 [32768, 384], P(('dp', 'tensor')), may hold values from 0 to 255
- key_codes: int32 [32768, 384], P(('dp', 'tensor')), may hold values from 0 to 255
- key_live: int32 [32768], P(('dp', 'tensor')), may hold values 0 or 1
- seq_lengths: int32 [128, 4], P(('dp', 'tensor')), may hold values from 1 to 128, 256 in all within a row
- out_grad: bfloat16 [32768, 768], P(('dp', 'tensor')), may hold values from -6 to 6
Outputs:
- block_output: bfloat16 [32768, 768], P(('dp', 'tensor'))
- input_grad: float32 [32768, 768], P(('dp', 'tensor'))
- grad_w_value: float32 [768, 768], replicated
- grad_b_value: float32 [768], replicated
- grad_conv_kernel: float32 [65, 768], replicated
- grad_w_out: float32 [768, 768], replicated
- grad_b_out: float32 [768], replicated
- grad_gain_attn: float32 [768], replicated
- grad_shift_attn: float32 [768], replicated
- grad_w_up: float32 [768, 3072], P(None, 'tensor')
- grad_b_up: float32 [3072], P('tensor')
- grad_w_down: float32 [3072, 768], P('tensor')
- grad_b_down: float32 [768], replicated
- grad_gain_ffn: float32 [768], replicated
- grad_shift_ffn: float32 [768], replicated
Inputs may be any that keep to these rules, and one draw needn't show every extreme that they name: `seq_lengths`: each item's lengths sum to 256; the longest is 128. `key_live`: 1 marks a live key, 0 a padded one. `query_codes`: column h * 32 + s holds head h's code in hash set s. `key_codes`: column h * 32 + s holds head h's code in hash set s.
All inputs are finite; a program needn't handle non-finite values. No bound on the sum of `key_live` on one device may be relied on, other than what follows from the above.
Results may differ from a plain program's by a relative error of at most 0.02.
Values may be sent and summed in bfloat16 or wider, within the bound.
No kernel may reach another device: no remote copies, remote signals or barrier semaphores. Data moves between devices by JAX's collectives and lax.ppermute only.
A program may use at most 128 MiB of HBM per device.

v0:
```python
from functools import partial
import jax
import jax.numpy as jnp
from jax import lax
from jax.sharding import PartitionSpec as P

HEADS = 12
SETS = 32
BUCKETS = 256


def dot_last(former, latter):
    return lax.dot_general(
        former, latter, (((1,), (1,)), ((), ())), preferred_element_type=jnp.float32
    )


def dot_first(former, latter):
    return lax.dot_general(
        former, latter, (((0,), (0,)), ((), ())), preferred_element_type=jnp.float32
    )


def layer_norm(residual, gain_vec, shift_vec):
    average = jnp.mean(residual, axis=-1, keepdims=True)
    centred = residual - average
    variance = jnp.mean(centred * centred, axis=-1, keepdims=True)
    return centred * lax.rsqrt(variance + 1e-05) * gain_vec + shift_vec


def head_norm(mixed, head_count, head_dim):
    grouped = mixed.reshape(mixed.shape[0], head_count, head_dim)
    scaling = lax.rsqrt(jnp.mean(grouped * grouped, axis=-1, keepdims=True) + 1e-06)
    return (grouped * scaling).reshape(mixed.shape)


def gelu_exact(pre_act):
    return jax.nn.gelu(pre_act, approximate=False)


def depth_conv(values, kernel, segment):
    taps = kernel.shape[0]
    margin = taps // 2
    length = values.shape[0]
    padded = jnp.pad(values, ((margin, margin), (0, 0)))
    seg_padded = jnp.pad(segment, (margin, margin), constant_values=-1)
    running = jnp.zeros_like(values)
    for offset in range(taps):
        joined = (seg_padded[offset : offset + length] == segment).astype(jnp.float32)[:, None]
        running = running + padded[offset : offset + length] * joined * kernel[offset][None, :]
    return running


def conv_back(grad_out, values, kernel, segment):
    taps = kernel.shape[0]
    margin = taps // 2
    length = values.shape[0]
    padded = jnp.pad(values, ((margin, margin), (0, 0)))
    grad_padded = jnp.pad(grad_out, ((margin, margin), (0, 0)))
    seg_padded = jnp.pad(segment, (margin, margin), constant_values=-1)
    value_grad = jnp.zeros_like(values)
    tap_rows = []
    for offset in range(taps):
        joined = (seg_padded[offset : offset + length] == segment).astype(jnp.float32)[:, None]
        tap_rows.append(jnp.sum(grad_out * joined * padded[offset : offset + length], axis=0))
        mirror = 2 * margin - offset
        back_joined = (seg_padded[mirror : mirror + length] == segment).astype(jnp.float32)[:, None]
        value_grad = (
            value_grad
            + grad_padded[mirror : mirror + length] * back_joined * kernel[offset][None, :]
        )
    return (value_grad, jnp.stack(tap_rows, axis=0))


def body(
    block_input,
    w_value,
    b_value,
    conv_kernel,
    w_out,
    b_out,
    gain_attn,
    shift_attn,
    w_up,
    b_up,
    w_down,
    b_down,
    gain_ffn,
    shift_ffn,
    query_codes,
    key_codes,
    key_live,
    seq_lengths,
    out_grad,
):
    length = block_input.shape[0]
    model_width = block_input.shape[1]
    head_dim = model_width // HEADS
    live_keys = key_live.astype(jnp.float32)[:, None]
    seq_ends = jnp.cumsum(seq_lengths[0], dtype=jnp.int32)
    positions = jnp.arange(length, dtype=jnp.int32)
    segment = jnp.sum(
        (seq_ends[None, :] <= positions[:, None]).astype(jnp.int32), axis=1, dtype=jnp.int32
    )
    query_heads = query_codes.reshape(length, HEADS, SETS).transpose(1, 0, 2)
    key_heads = key_codes.reshape(length, HEADS, SETS).transpose(1, 0, 2)
    joined = (segment[:, None] == segment[None, :]).astype(jnp.float32)
    bucket_ids = jnp.arange(BUCKETS, dtype=jnp.int32)

    def head_counts(pair):
        query_set, key_set = pair
        query_hot = (
            (query_set[:, :, None] == bucket_ids[None, None, :])
            .astype(jnp.bfloat16)
            .reshape(length, SETS * BUCKETS)
        )
        key_hot = (
            (key_set[:, :, None] == bucket_ids[None, None, :])
            .astype(jnp.bfloat16)
            .reshape(length, SETS * BUCKETS)
        )
        counts = dot_last(query_hot, key_hot)
        return (counts * joined / SETS).astype(jnp.bfloat16)

    collide = lax.map(head_counts, (query_heads, key_heads))
    kernel_f = conv_kernel.astype(jnp.float32)
    value_pre = jnp.dot(block_input, w_value, preferred_element_type=jnp.float32) + b_value.astype(
        jnp.float32
    )
    values = value_pre.astype(jnp.bfloat16)
    masked = values.astype(jnp.float32) * live_keys
    masked_low = masked.astype(jnp.bfloat16)
    mixed = jnp.einsum(
        "hij,jhd->ihd",
        collide,
        masked_low.reshape(length, HEADS, head_dim),
        preferred_element_type=jnp.float32,
    ).reshape(length, model_width)
    normed, norm_back = jax.vjp(partial(head_norm, head_count=HEADS, head_dim=head_dim), mixed)
    context = (normed + depth_conv(masked, kernel_f, segment)).astype(jnp.bfloat16)
    attended = jnp.dot(context, w_out, preferred_element_type=jnp.float32) + b_out.astype(
        jnp.float32
    )
    first, first_back = jax.vjp(
        layer_norm,
        block_input.astype(jnp.float32) + attended,
        gain_attn.astype(jnp.float32),
        shift_attn.astype(jnp.float32),
    )
    first_low = first.astype(jnp.bfloat16)
    gathered = lax.all_gather(first_low, "tensor", axis=0, tiled=True)
    upper = jnp.dot(gathered, w_up, preferred_element_type=jnp.float32) + b_up.astype(jnp.float32)
    active_f, gelu_back = jax.vjp(gelu_exact, upper)
    active = active_f.astype(jnp.bfloat16)
    branch = lax.psum_scatter(
        jnp.dot(active, w_down, preferred_element_type=jnp.float32).astype(jnp.bfloat16),
        "tensor",
        scatter_dimension=0,
        tiled=True,
    ).astype(jnp.float32) + b_down.astype(jnp.float32)
    block_output, second_back = jax.vjp(
        layer_norm, first + branch, gain_ffn.astype(jnp.float32), shift_ffn.astype(jnp.float32)
    )
    grad_second, grad_gain_ffn, grad_shift_ffn = second_back(out_grad.astype(jnp.float32))
    branch_grad = grad_second.astype(jnp.bfloat16)
    grad_b_down = jnp.sum(branch_grad.astype(jnp.float32), axis=0)
    grad_rows_all = lax.all_gather(branch_grad, "tensor", axis=0, tiled=True)
    active_grad = dot_last(grad_rows_all, w_down)
    grad_w_down = dot_first(active, grad_rows_all)
    upper_grad = gelu_back(active_grad)[0].astype(jnp.bfloat16)
    grad_w_up = dot_first(gathered, upper_grad)
    grad_b_up = jnp.sum(upper_grad.astype(jnp.float32), axis=0)
    first_grad_ffn = lax.psum_scatter(
        dot_last(upper_grad, w_up).astype(jnp.bfloat16), "tensor", scatter_dimension=0, tiled=True
    ).astype(jnp.float32)
    first_grad = grad_second + first_grad_ffn
    resid_grad, grad_gain_attn, grad_shift_attn = first_back(first_grad)
    attended_grad = resid_grad.astype(jnp.bfloat16)
    grad_b_out = jnp.sum(attended_grad.astype(jnp.float32), axis=0)
    grad_w_out = dot_first(context, attended_grad)
    context_grad = dot_last(attended_grad, w_out)
    mixed_grad = norm_back(context_grad)[0].astype(jnp.bfloat16)
    conv_value_grad, grad_kernel = conv_back(context_grad, masked, kernel_f, segment)
    masked_att = jnp.einsum(
        "hij,ihd->jhd",
        collide,
        mixed_grad.reshape(length, HEADS, head_dim),
        preferred_element_type=jnp.float32,
    ).reshape(length, model_width)
    value_grad = ((masked_att + conv_value_grad) * live_keys).astype(jnp.bfloat16)
    grad_b_value = jnp.sum(value_grad.astype(jnp.float32), axis=0)
    grad_w_value = dot_first(block_input, value_grad)
    input_grad = resid_grad + dot_last(value_grad, w_value)
    grad_w_up, grad_w_down, grad_b_up = (
        lax.psum(grad_w_up.astype(jnp.bfloat16), "dp").astype(jnp.float32),
        lax.psum(grad_w_down.astype(jnp.bfloat16), "dp").astype(jnp.float32),
        lax.psum(grad_b_up.astype(jnp.bfloat16), "dp").astype(jnp.float32),
    )
    (
        grad_w_value,
        grad_b_value,
        grad_kernel,
        grad_w_out,
        grad_b_out,
        grad_gain_attn,
        grad_shift_attn,
        grad_b_down,
        grad_gain_ffn,
        grad_shift_ffn,
    ) = lax.psum(
        (
            grad_w_value,
            grad_b_value,
            grad_kernel,
            grad_w_out,
            grad_b_out,
            grad_gain_attn,
            grad_shift_attn,
            grad_b_down,
            grad_gain_ffn,
            grad_shift_ffn,
        ),
        ("dp", "tensor"),
    )
    return (
        block_output.astype(jnp.bfloat16),
        input_grad,
        grad_w_value,
        grad_b_value,
        grad_kernel,
        grad_w_out,
        grad_b_out,
        grad_gain_attn,
        grad_shift_attn,
        grad_w_up,
        grad_b_up,
        grad_w_down,
        grad_b_down,
        grad_gain_ffn,
        grad_shift_ffn,
    )


def solution(mesh):
    return jax.shard_map(
        body,
        mesh=mesh,
        in_specs=(
            P(("dp", "tensor"), None),
            P(),
            P(),
            P(),
            P(),
            P(),
            P(),
            P(),
            P(None, "tensor"),
            P("tensor"),
            P("tensor", None),
            P(),
            P(),
            P(),
            P(("dp", "tensor"), None),
            P(("dp", "tensor"), None),
            P(("dp", "tensor")),
            P(("dp", "tensor"), None),
            P(("dp", "tensor"), None),
        ),
        out_specs=(
            P(("dp", "tensor"), None),
            P(("dp", "tensor"), None),
            P(),
            P(),
            P(),
            P(),
            P(),
            P(),
            P(),
            P(None, "tensor"),
            P("tensor"),
            P("tensor", None),
            P(),
            P(),
            P(),
        ),
        check_vma=False,
    )
```

profile of v0, /device:TPU:1, one launch (start us, length us, event | category | flops | bytes accessed | tf_op | source)
XLA Modules:
  0.0 701.4 jit_solution(10940862884612107198)
XLA Ops:
  17.3 43.1 %while.12 = (s32[]{:T(128)}, bf16[12,256,256]{2,1,0:T(8,128)(2,1)}, s32[12,256,32]{1,2,0:T(8,128)S(1)}, s32[12,256,32]{1,2,0:T(8,128)S(1)}, s32[256]{0:T(256)S(1)}, /*index=5*/s32[]{:T(128)}) while((s32[]{:T(128)}, bf16[12,256,256]{2,1,0:T(8,128)(2,1)}, s32[12,256,32]{1,2,0:T(8,128)S(1)}, s32[12,256,32]{1,2,0:T(8,128)S(1)}, ...), condition=%wide.region_3.4_spmd.clone.clone, body=%wide.region_2.3_spmd.clone.clone.sunk | while | flops 1078198272 | bytes 330313 | solution.py:125
  17.4 3.6 fusion.266
  21.0 3.6 fusion.266
  24.6 3.6 fusion.266
  28.1 3.6 fusion.266
  35.3 3.6 fusion.266
  42.5 3.6 fusion.266
  46.1 3.6 fusion.266
  53.3 3.6 fusion.266
  66.3 11.6 %add_convert_fusion.2 = bf16[256,768]{1,0:T(8,128)(2,1)S(1)} fusion(f32[256,768]{1,0:T(8,128)S(1)} %copy.51, f32[256,768]{1,0:T(8,128)S(1)} %get-tuple-element.368, f32[768]{0:T(1024)} %get-tuple-element.198, f32[256]{0:T(256)} %get-tuple-element.366, f32[768]{0:T(1024)} %get-tuple-element.199, f32[256]{0:T(256)} %get-tuple-element.365, ...), kind=kLoop, calls=%fused_computation.456 | loop fusion | flops 38338560 | bytes 2231296 | tf_op jit(solution)/shard_map/convert_element_type | solution.py:140
  83.6 11.4 %reduce-scatter.3.cloned.1.call-start = ((), (), s32[]{:S(2)}) async-start(), calls=%async_computation.3 | async-start | bytes 3538944 | tf_op jit(solution)/shard_map/reduce_scatter | solution.py:155
  96.2 53.2 %all-gather.3.cloned.1.call-done = bf16[2048,768]{1,0:T(8,128)(2,1)} async-done(((bf16[256,768]{1,0:T(8,128)(2,1)}), bf16[2048,768]{1,0:T(8,128)(2,1)}) %all-gather.3.cloned.1.call-update) | async-done | bytes 3145744 | tf_op jit(solution)/shard_map/all_gather | solution.py:151
  149.4 11.6 %multiply_convert_fusion = (bf16[2048,384]{1,0:T(8,128)(2,1)S(1)}, f32[2048,384]{1,0:T(8,128)}, f32[2048,384]{1,0:T(8,128)}) fusion(f32[384]{0:T(512)} %convert_element_type.529, bf16[2048,768]{1,0:T(8,128)(2,1)} %all-gather.3.cloned.1.call-done, bf16[768,384]{1,0:T(8,128)(2,1)} %param.29), kind=kOutput, calls=%fused_computation.148 | convolution fusion | flops 1259864064 | bytes 11601408 | tf_op jit(solution)/shard_map/dot_general | solution.py:152
  169.5 72.7 %reduce-scatter.3.cloned.1.call-done = bf16[256,768]{1,0:T(8,128)(2,1)} async-done(((bf16[2048,768]{1,0:T(8,128)(2,1)}), bf16[256,768]{1,0:T(8,128)(2,1)}) %reduce-scatter.3.cloned.1.call-update) | async-done | bytes 393232 | tf_op jit(solution)/shard_map/reduce_scatter | solution.py:155
  249.4 62.5 %all-gather.5.cloned.1.call-done = bf16[2048,768]{1,0:T(8,128)(2,1)} async-done(((bf16[256,768]{1,0:T(8,128)(2,1)}), bf16[2048,768]{1,0:T(8,128)(2,1)}) %all-gather.5.cloned.1.call-update) | async-done | bytes 3145744 | tf_op jit(solution)/shard_map/all_gather | solution.py:167
  311.9 7.3 %fusion.230 = (bf16[384]{0:T(512)(128)(2,1)}, bf16[2048,384]{1,0:T(8,128)(2,1)S(1)}) fusion(f32[2048,384]{1,0:T(8,128)} %get-tuple-element.299, f32[2048,384]{1,0:T(8,128)} %get-tuple-element.373, bf16[2048,768]{1,0:T(8,128)(2,1)} %all-gather.5.cloned.1.call-done, bf16[384,768]{1,0:T(8,128)(2,1)} %param.31), kind=kOutput, calls=%fused_computation.674 | convolution fusion | flops 1219755648 | bytes 11600640 | tf_op jit(solution)/shard_map/dot_general | solution.py:13
  324.0 4.8 convolution_convert_fusion.2
  331.5 69.1 %reduce-scatter.5.cloned.1.call-done = bf16[256,768]{1,0:T(8,128)(2,1)} async-done(((bf16[2048,768]{1,0:T(8,128)(2,1)}), bf16[256,768]{1,0:T(8,128)(2,1)}) %reduce-scatter.5.cloned.1.call-update) | async-done | bytes 393232 | tf_op jit(solution)/shard_map/reduce_scatter | solution.py:173
  451.9 5.8 stack.263
  457.7 11.7 %convert_reduce_fusion.3 = (f32[768]{0:T(1024)S(1)}, bf16[256,768]{1,0:T(8,128)(2,1)S(1)}) fusion(f32[256]{0:T(256)} %copy-done.110, f32[256,768]{1,0:T(8,128)S(1)} %copy.53, f32[768]{0:T(1024)} %get-tuple-element.198, f32[256]{0:T(256)} %get-tuple-element.303, f32[768]{0:T(1024)} %get-tuple-element.199, f32[256]{0:T(256)} %get-tuple-element.321, ...), kind=kLoop, calls=%fused_computation.446 | loop fusion | flops 38927616 | bytes 2235392 | tf_op jit(solution)/shard_map/reduce_sum | solution.py:191
  472.0 28.5 %psum.99 = bf16[384]{0:T(512)(128)(2,1)S(1)} all-reduce(bf16[384]{0:T(512)(128)(2,1)S(1)} %copy-done.120), channel_id=1, replica_groups=mesh['dp'=16,'tensor'=8] {'dp'}, use_global_device_ids=true, to_apply=%region_94.95 | all-reduce | flops 384 | bytes 1536 | tf_op jit(solution)/shard_map/psum | solution.py:197
  501.1 22.6 %all-reduce.11.cloned.1.call-done = (bf16[768,384]{1,0:T(8,128)(2,1)}, bf16[384,768]{1,0:T(8,128)(2,1)}) async-done(((bf16[768,384]{1,0:T(8,128)(2,1)}, bf16[384,768]{1,0:T(8,128)(2,1)}), (bf16[768,384]{1,0:T(8,128)(2,1)}, bf16[384,768]{1,0:T(8,128)(2,1)})) %all-reduce.11.cloned.1.call-update) | async-done | bytes 1179664 | tf_op jit(solution)/shard_map/psum | solution.py:195
  528.0 68.4 %all-reduce.3 = (f32[768]{0:T(1024)}, f32[768]{0:T(1024)}, f32[768]{0:T(1024)}, f32[768]{0:T(1024)}, f32[768]{0:T(1024)}, /*index=5*/f32[768]{0:T(1024)}, f32[768]{0:T(1024)}) all-reduce(f32[768]{0:T(1024)S(1)} %get-tuple-element.290, f32[768]{0:T(1024)S(1)} %copy-done.37, ...), channel_id=1, replica_groups=mesh['dp'=16,'tensor'=8] {'dp','tensor'}, use_global_device_ids=true, to_apply=%region_18.19 | all-reduce | flops 5376 | bytes 43008 | tf_op jit(solution)/shard_map/psum | solution.py:210
  597.9 89.3 %all-reduce.9.cloned.1.call-done = (f32[768,768]{0,1:T(8,128)}, f32[65,768]{1,0:T(8,128)}, f32[768,768]{1,0:T(8,128)}) async-done(((f32[768,768]{0,1:T(8,128)}, f32[65,768]{1,0:T(8,128)}, f32[768,768]{1,0:T(8,128)}), (f32[768,768]{0,1:T(8,128)}, f32[65,768]{1,0:T(8,128)}, f32[768,768]{1,0:T(8,128)})) %all-reduce.9.cloned.1.call-update) | async-done | bytes 4918288 | tf_op jit(solution)/shard_map/psum | solution.py:210
  (413 shorter events, 125.8 us)
Async XLA Ops:
  7.2 53.3 %copy-start = (bf16[768,768]{1,0:T(8,128)(2,1)S(1)}, bf16[768,768]{1,0:T(8,128)(2,1)}, u32[]{:S(2)}) copy-start(bf16[768,768]{1,0:T(8,128)(2,1)} %param.22) | copy-start | bytes 3538948
  7.2 142.2 %all-gather.3.cloned.1.call-start = ((), (), s32[]{:S(2)}) async-start(), calls=%async_computation.2 | async-start | bytes 3538944 | tf_op jit(solution)/shard_map/all_gather | solution.py:151
  17.3 43.1 %copy-start.119 = (s32[256]{0:T(256)S(1)}, s32[256]{0:T(256)}, u32[]{:S(2)}) copy-start(s32[256]{0:T(256)} %param.37) | copy-start | bytes 3076
  17.3 43.1 %copy-start.116 = (bf16[768]{0:T(1024)(128)(2,1)S(1)}, bf16[768]{0:T(1024)(128)(2,1)}, u32[]{:S(2)}) copy-start(bf16[768]{0:T(1024)(128)(2,1)} %param.23) | copy-start | bytes 4612
  17.3 43.1 %copy-start.6 = (bf16[256,768]{1,0:T(8,128)(2,1)S(1)}, bf16[256,768]{1,0:T(8,128)(2,1)}, u32[]{:S(2)}) copy-start(bf16[256,768]{1,0:T(8,128)(2,1)} %param.21) | copy-start | bytes 1179652
  83.6 158.7 %reduce-scatter.3.cloned.1.call-start = ((), (), s32[]{:S(2)}) async-start(), calls=%async_computation.3 | async-start | bytes 3538944 | tf_op jit(solution)/shard_map/reduce_scatter | solution.py:155
  165.6 146.3 %all-gather.5.cloned.1.call-start = ((), (), s32[]{:S(2)}) async-start(), calls=%async_computation.4 | async-start | bytes 3538944 | tf_op jit(solution)/shard_map/all_gather | solution.py:167
  249.3 151.3 %reduce-scatter.5.cloned.1.call-start = ((), (), s32[]{:S(2)}) async-start(), calls=%async_computation.5 | async-start | bytes 3538944 | tf_op jit(solution)/shard_map/reduce_scatter | solution.py:173
  323.9 199.8 %all-reduce.11.cloned.1.call-start = ((), (), s32[]{:S(2)}) async-start(), calls=%async_computation.7 | async-start | bytes 2359296 | tf_op jit(solution)/shard_map/psum | solution.py:195
  331.4 355.7 %all-reduce.9.cloned.1.call-start = ((), (), s32[]{:S(2)}) async-start(), calls=%async_computation.6 | async-start | bytes 9879552 | tf_op jit(solution)/shard_map/psum | solution.py:210
  429.2 21.2 %copy-start.42 = (f32[768]{0:T(1024)S(1)}, f32[768]{0:T(1024)}, u32[]{:S(2)}) copy-start(f32[768]{0:T(1024)} %get-tuple-element.186) | copy-start | bytes 9220
  429.2 21.2 %copy-start.41 = (f32[768]{0:T(1024)S(1)}, f32[768]{0:T(1024)}, u32[]{:S(2)}) copy-start(f32[768]{0:T(1024)} %get-tuple-element.185) | copy-start | bytes 9220
  429.2 21.3 %copy-start.40 = (f32[768]{0:T(1024)S(1)}, f32[768]{0:T(1024)}, u32[]{:S(2)}) copy-start(f32[768]{0:T(1024)} %get-tuple-element.184) | copy-start | bytes 9220
  429.2 21.3 %copy-start.39 = (f32[768]{0:T(1024)S(1)}, f32[768]{0:T(1024)}, u32[]{:S(2)}) copy-start(f32[768]{0:T(1024)} %get-tuple-element.183) | copy-start | bytes 9220
  429.2 21.3 %copy-start.38 = (f32[768]{0:T(1024)S(1)}, f32[768]{0:T(1024)}, u32[]{:S(2)}) copy-start(f32[768]{0:T(1024)} %get-tuple-element.182) | copy-start | bytes 9220
  430.6 38.8 %copy-start.7 = (bf16[256,768]{1,0:T(8,128)(2,1)S(1)}, bf16[256,768]{1,0:T(8,128)(2,1)}, u32[]{:S(2)}) copy-start(bf16[256,768]{1,0:T(8,128)(2,1)} %param.21) | copy-start | bytes 1179652
  471.3 56.7 %copy-start.32 = (f32[768]{0:T(1024)S(1)}, f32[768]{0:T(1024)}, u32[]{:S(2)}) copy-start(f32[768]{0:T(1024)} %get-tuple-element.193) | copy-start | bytes 9220
  471.3 56.7 %copy-start.33 = (f32[768]{0:T(1024)S(1)}, f32[768]{0:T(1024)}, u32[]{:S(2)}) copy-start(f32[768]{0:T(1024)} %get-tuple-element.196) | copy-start | bytes 9220
  471.3 56.7 %copy-start.34 = (f32[768]{0:T(1024)S(1)}, f32[768]{0:T(1024)}, u32[]{:S(2)}) copy-start(f32[768]{0:T(1024)} %get-tuple-element.286) | copy-start | bytes 9220
  471.3 56.7 %copy-start.35 = (f32[768]{0:T(1024)S(1)}, f32[768]{0:T(1024)}, u32[]{:S(2)}) copy-start(f32[768]{0:T(1024)} %get-tuple-element.126) | copy-start | bytes 9220
  471.3 56.7 %copy-start.36 = (f32[768]{0:T(1024)S(1)}, f32[768]{0:T(1024)}, u32[]{:S(2)}) copy-start(f32[768]{0:T(1024)} %get-tuple-element.195) | copy-start | bytes 9220
  471.4 56.7 %copy-start.37 = (f32[768]{0:T(1024)S(1)}, f32[768]{0:T(1024)}, u32[]{:S(2)}) copy-start(f32[768]{0:T(1024)} %get-tuple-element.288) | copy-start | bytes 9220
  471.4 125.1 %copy-start.3 = (f32[256,768]{1,0:T(8,128)S(1)}, f32[256,768]{1,0:T(8,128)}, u32[]{:S(2)}) copy-start(f32[256,768]{1,0:T(8,128)} %copy-done.2) | copy-start | bytes 2359300
  471.4 125.1 %copy-start.115 = (f32[256]{0:T(256)S(1)}, f32[256]{0:T(256)}, u32[]{:S(2)}) copy-start(f32[256]{0:T(256)} %copy-done.114) | copy-start | bytes 3076
  (106 other events, 1160.3 us)
Sparse Core Ops, SparseCore 0:
  83.7 65.6 all-gather.2
  165.7 76.4 reduce-scatter.2
  249.5 62.4 all-gather.4
  324.0 76.5 reduce-scatter.4
  403.6 120.0 all-reduce.10
  529.7 157.4 all-reduce.8
where the time goes:
time: 710 us; the launch traced here: 701 us
  waiting for transfers between devices  369 us (52%)
  blocking collectives  97 us (14%)
  matrix products  88.4 us (12%)
  other arithmetic  70.4 us (10%)
  local copies, waits for them, and re-layouts  48.2 us (7%)
  between operations  16.4 us (2%)
  starting transfers between devices  11.6 us (2%)
    psum x1, waiting for transfers between devices, body(): lax.psum((grad_w_value, grad_b_value, grad_kernel, grad_w_out, grad_b_out...  89.3 us
    reduce_scatter x1, waiting for transfers between devices, body(): lax.psum_scatter(jnp.dot(active, w_down, preferred_element_type=jnp.float...  72.7 us
    reduce_scatter x1, waiting for transfers between devices, body(): lax.psum_scatter(dot_last(upper_grad, w_up).astype(jnp.bfloat16), 'tensor...  69.1 us
    psum x1, blocking collectives, body(): lax.psum((grad_w_value, grad_b_value, grad_kernel, grad_w_out, grad_b_out...  68.4 us
    all_gather x1, waiting for transfers between devices, body(): grad_rows_all = lax.all_gather(branch_grad, 'tensor', axis=0, tiled=True)  62.5 us
    dot_general x16, matrix products, dot_last(): lax.dot_general(former, latter, (((1,), (1,)), ((), ())), preferred_eleme...  56.4 us
    all_gather x1, waiting for transfers between devices, body(): gathered = lax.all_gather(first_low, 'tensor', axis=0, tiled=True)  53.2 us
    psum x1, blocking collectives, body(): lax.psum(grad_b_up.astype(jnp.bfloat16), 'dp').astype(jnp.float32)  28.5 us
  transfers between devices with their start and end apart: 6, of which 6 were waited for; matrix products, arithmetic and copies ran while one was open for 12% of the time, Pallas kernels for 0%

commit v1 on v0

--- a/solution.py
+++ b/solution.py
@@ -3,10 +3,16 @@
 import jax.numpy as jnp
 from jax import lax
 from jax.sharding import PartitionSpec as P
+from jax.lax import psum
 
 HEADS = 12
 SETS = 32
 BUCKETS = 256
+
+
+def begin_the_group(u):
+    h_now = psum(psum(u, "tensor"), "dp")
+    return h_now
 
 
 def dot_last(former, latter):
@@ -207,7 +213,7 @@
         grad_b_down,
         grad_gain_ffn,
         grad_shift_ffn,
-    ) = lax.psum(
+    ) = begin_the_group(
         (
             grad_w_value,
             grad_b_value,
@@ -219,8 +225,7 @@
             grad_b_down,
             grad_gain_ffn,
             grad_shift_ffn,
-        ),
-        ("dp", "tensor"),
+        )
     )
     return (
         block_output.astype(jnp.bfloat16),

time: 710 us -> 898 us (1.26)
  waiting for transfers between devices: 369 us -> 524 us
  local copies, waits for them, and re-layouts: 48.2 us -> 70.4 us
  blocking collectives: 97 us -> 118 us
  starting transfers between devices: 11.6 us -> 1.14 us
    psum x1, waiting for transfers between devices: 22.6 us -> 93.8 us  [body(): lax.psum(grad_w_up.astype(jnp.bfloat16), 'dp').astype(jnp.float32)]
    psum x1 -> x2, waiting for transfers between devices: 89.3 us -> 154 us  [begin_the_group(): h_now = psum(psum(u, 'tensor'), 'dp')]
    another operation x66, local copies, waits for them, and re-layouts: 25 us -> 48 us  [conv_back(): return (value_grad, jnp.stack(tap_rows, axis=0))]
    psum x1 -> x2, blocking collectives: 68.4 us -> 91 us  [begin_the_group(): h_now = psum(psum(u, 'tensor'), 'dp')]
    all_gather x1, waiting for transfers between devices: 53.2 us -> 64 us  [body(): gathered = lax.all_gather(first_low, 'tensor', axis=0, tiled=True)]
    reduce_scatter x1, starting transfers between devices: 11.4 us -> 0.51 us  [body(): lax.psum_scatter(jnp.dot(active, w_down, preferred_element_type=jnp.float...]
  transfers between devices with their start and end apart: 6 -> 7, of which waited for: 6 -> 7; matrix products, arithmetic and copies ran while one was open for 12% -> 2% of each run, Pallas kernels for 0% -> 0%
where the time goes in v1:
time: 898 us; the launch traced here: 888 us
  waiting for transfers between devices  524 us (58%)
  blocking collectives  118 us (13%)
  matrix products  88.3 us (10%)
  other arithmetic  70.7 us (8%)
  local copies, waits for them, and re-layouts  70.4 us (8%)
  between operations  15.4 us (2%)
    psum x2, waiting for transfers between devices, begin_the_group(): h_now = psum(psum(u, 'tensor'), 'dp')  154 us
    psum x1, waiting for transfers between devices, body(): lax.psum(grad_w_up.astype(jnp.bfloat16), 'dp').astype(jnp.float32)  93.8 us
    psum x2, blocking collectives, begin_the_group(): h_now = psum(psum(u, 'tensor'), 'dp')  91 us
    reduce_scatter x1, waiting for transfers between devices, body(): lax.psum_scatter(dot_last(upper_grad, w_up).astype(jnp.bfloat16), 'tensor...  76.5 us
    reduce_scatter x1, waiting for transfers between devices, body(): lax.psum_scatter(jnp.dot(active, w_down, preferred_element_type=jnp.float...  72.7 us
    all_gather x1, waiting for transfers between devices, body(): gathered = lax.all_gather(first_low, 'tensor', axis=0, tiled=True)  64 us
    all_gather x1, waiting for transfers between devices, body(): grad_rows_all = lax.all_gather(branch_grad, 'tensor', axis=0, tiled=True)  62.5 us
    dot_general x16, matrix products, dot_last(): lax.dot_general(former, latter, (((1,), (1,)), ((), ())), preferred_eleme...  56.4 us
  transfers between devices with their start and end apart: 7, of which 7 were waited for; matrix products, arithmetic and copies ran while one was open for 2% of the time, Pallas kernels for 0%

profile of v1, /device:TPU:1, one launch (start us, length us, event | category | flops | bytes accessed | tf_op | source)
XLA Modules:
  0.0 888.1 jit_solution(9586789266774734349)
XLA Ops:
  17.3 43.1 %while.12 = (s32[]{:T(128)}, bf16[12,256,256]{2,1,0:T(8,128)(2,1)}, s32[12,256,32]{1,2,0:T(8,128)S(1)}, s32[12,256,32]{1,2,0:T(8,128)S(1)}, s32[256]{0:T(256)S(1)}, /*index=5*/s32[]{:T(128)}) while((s32[]{:T(128)}, bf16[12,256,256]{2,1,0:T(8,128)(2,1)}, s32[12,256,32]{1,2,0:T(8,128)S(1)}, s32[12,256,32]{1,2,0:T(8,128)S(1)}, ...), condition=%wide.region_3.4_spmd.clone.clone, body=%wide.region_2.3_spmd.clone.clone.sunk | while | flops 1078198272 | bytes 330313 | solution.py:131
  17.4 3.6 fusion.266
  24.5 3.6 fusion.266
  28.1 3.6 fusion.266
  35.3 3.6 fusion.266
  42.5 3.6 fusion.266
  49.7 3.6 fusion.266
  53.2 3.6 fusion.266
  66.3 11.6 %add_convert_fusion.2 = bf16[256,768]{1,0:T(8,128)(2,1)S(1)} fusion(f32[256,768]{1,0:T(8,128)S(1)} %copy.51, f32[256,768]{1,0:T(8,128)S(1)} %get-tuple-element.378, f32[768]{0:T(1024)} %get-tuple-element.198, f32[256]{0:T(256)} %get-tuple-element.376, f32[768]{0:T(1024)} %get-tuple-element.199, f32[256]{0:T(256)} %get-tuple-element.375, ...), kind=kLoop, calls=%fused_computation.456 | loop fusion | flops 38338560 | bytes 2231296 | tf_op jit(solution)/shard_map/convert_element_type | solution.py:146
  85.4 64.0 %all-gather.3.cloned.1.call-done = bf16[2048,768]{1,0:T(8,128)(2,1)} async-done(((bf16[256,768]{1,0:T(8,128)(2,1)}), bf16[2048,768]{1,0:T(8,128)(2,1)}) %all-gather.3.cloned.1.call-update) | async-done | bytes 3145744 | tf_op jit(solution)/shard_map/all_gather | solution.py:157
  149.4 11.5 %multiply_convert_fusion = (bf16[2048,384]{1,0:T(8,128)(2,1)S(1)}, f32[2048,384]{1,0:T(8,128)}, f32[2048,384]{1,0:T(8,128)}) fusion(f32[384]{0:T(512)} %convert_element_type.529, bf16[2048,768]{1,0:T(8,128)(2,1)} %all-gather.3.cloned.1.call-done, bf16[768,384]{1,0:T(8,128)(2,1)} %param.29), kind=kOutput, calls=%fused_computation.148 | convolution fusion | flops 1259864064 | bytes 11601408 | tf_op jit(solution)/shard_map/dot_general | solution.py:158
  169.5 72.7 %reduce-scatter.3.cloned.1.call-done = bf16[256,768]{1,0:T(8,128)(2,1)} async-done(((bf16[2048,768]{1,0:T(8,128)(2,1)}), bf16[256,768]{1,0:T(8,128)(2,1)}) %reduce-scatter.3.cloned.1.call-update) | async-done | bytes 393232 | tf_op jit(solution)/shard_map/reduce_scatter | solution.py:161
  249.4 62.5 %all-gather.5.cloned.1.call-done = bf16[2048,768]{1,0:T(8,128)(2,1)} async-done(((bf16[256,768]{1,0:T(8,128)(2,1)}), bf16[2048,768]{1,0:T(8,128)(2,1)}) %all-gather.5.cloned.1.call-update) | async-done | bytes 3145744 | tf_op jit(solution)/shard_map/all_gather | solution.py:173
  311.9 7.3 fusion.230
  324.2 76.5 %reduce-scatter.5.cloned.1.call-done = bf16[256,768]{1,0:T(8,128)(2,1)} async-done(((bf16[2048,768]{1,0:T(8,128)(2,1)}), bf16[256,768]{1,0:T(8,128)(2,1)}) %reduce-scatter.5.cloned.1.call-update) | async-done | bytes 393232 | tf_op jit(solution)/shard_map/reduce_scatter | solution.py:179
  431.6 12.1 %convert_reduce_fusion.3 = (f32[768]{0:T(1024)S(1)}, bf16[256,768]{1,0:T(8,128)(2,1)S(1)}) fusion(f32[256]{0:T(256)} %copy-done.76, f32[256,768]{1,0:T(8,128)S(1)} %copy.53, f32[768]{0:T(1024)} %get-tuple-element.198, f32[256]{0:T(256)} %get-tuple-element.313, f32[768]{0:T(1024)} %get-tuple-element.199, f32[256]{0:T(256)} %get-tuple-element.331, ...), kind=kLoop, calls=%fused_computation.446 | loop fusion | flops 38927616 | bytes 2235392 | tf_op jit(solution)/shard_map/reduce_sum | solution.py:197
  487.9 5.8 stack.263
  494.0 4.7 convolution_convert_fusion.2
  501.4 114.9 %all-reduce.14.cloned.1.call-done = (f32[768,768]{0,1:T(8,128)}, f32[65,768]{1,0:T(8,128)}, f32[768,768]{1,0:T(8,128)}) async-done(((f32[768,768]{0,1:T(8,128)}, f32[65,768]{1,0:T(8,128)}, f32[768,768]{1,0:T(8,128)}), (f32[768,768]{0,1:T(8,128)}, f32[65,768]{1,0:T(8,128)}, f32[768,768]{1,0:T(8,128)})) %all-reduce.14.cloned.1.call-update) | async-done | bytes 4918288 | tf_op jit(solution)/shard_map/psum | solution.py:14
  616.4 27.3 %psum.176 = bf16[384]{0:T(512)(128)(2,1)S(1)} all-reduce(bf16[384]{0:T(512)(128)(2,1)S(1)} %copy-done.86), channel_id=1, replica_groups=mesh['dp'=16,'tensor'=8] {'dp'}, use_global_device_ids=true, to_apply=%region_101.102 | all-reduce | flops 384 | bytes 1536 | tf_op jit(solution)/shard_map/psum | solution.py:203
  644.4 93.8 %all-reduce.16.cloned.1.call-done = (bf16[768,384]{1,0:T(8,128)(2,1)}, bf16[384,768]{1,0:T(8,128)(2,1)}) async-done(((bf16[768,384]{1,0:T(8,128)(2,1)}, bf16[384,768]{1,0:T(8,128)(2,1)}), (bf16[768,384]{1,0:T(8,128)(2,1)}, bf16[384,768]{1,0:T(8,128)(2,1)})) %all-reduce.16.cloned.1.call-update) | async-done | bytes 1179664 | tf_op jit(solution)/shard_map/psum | solution.py:201
  742.5 34.6 %all-reduce.5 = (f32[768]{0:T(1024)S(1)}, f32[768]{0:T(1024)S(1)}, f32[768]{0:T(1024)S(1)}, f32[768]{0:T(1024)S(1)}, f32[768]{0:T(1024)S(1)}, /*index=5*/f32[768]{0:T(1024)S(1)}, f32[768]{0:T(1024)S(1)}) all-reduce(f32[768]{0:T(1024)S(1)} %get-tuple-element.300, ...), channel_id=1, replica_groups=mesh['dp'=16,'tensor'=8] {'tensor'}, use_global_device_ids=true, to_apply=%region_19.20 | all-reduce | flops 5376 | bytes 43008 | tf_op jit(solution)/shard_map/psum | solution.py:14
  777.1 56.4 %all-reduce.3 = (f32[768]{0:T(1024)}, f32[768]{0:T(1024)}, f32[768]{0:T(1024)}, f32[768]{0:T(1024)}, f32[768]{0:T(1024)}, /*index=5*/f32[768]{0:T(1024)}, f32[768]{0:T(1024)}) all-reduce(f32[768]{0:T(1024)S(1)} %get-tuple-element.282, f32[768]{0:T(1024)S(1)} %get-tuple-element.283, ...), channel_id=1, replica_groups=mesh['dp'=16,'tensor'=8] {'dp'}, use_global_device_ids=true, to_apply=%region_20.21 | all-reduce | flops 5376 | bytes 43008 | tf_op jit(solution)/shard_map/psum | solution.py:14
  834.9 39.1 %all-reduce.12.cloned.1.call-done = (f32[768,768]{0,1:T(8,128)}, f32[65,768]{1,0:T(8,128)}, f32[768,768]{1,0:T(8,128)}) async-done(((f32[768,768]{0,1:T(8,128)}, f32[65,768]{1,0:T(8,128)}, f32[768,768]{1,0:T(8,128)}), (f32[768,768]{0,1:T(8,128)}, f32[65,768]{1,0:T(8,128)}, f32[768,768]{1,0:T(8,128)})) %all-reduce.12.cloned.1.call-update) | async-done | bytes 4918288 | tf_op jit(solution)/shard_map/psum | solution.py:14
  (349 shorter events, 152.5 us)
Async XLA Ops:
  7.2 53.3 %copy-start = (bf16[768,768]{1,0:T(8,128)(2,1)S(1)}, bf16[768,768]{1,0:T(8,128)(2,1)}, u32[]{:S(2)}) copy-start(bf16[768,768]{1,0:T(8,128)(2,1)} %param.22) | copy-start | bytes 3538948
  7.2 142.2 %all-gather.3.cloned.1.call-start = ((), (), s32[]{:S(2)}) async-start(), calls=%async_computation.2 | async-start | bytes 3538944 | tf_op jit(solution)/shard_map/all_gather | solution.py:157
  17.3 43.1 %copy-start.85 = (s32[256]{0:T(256)S(1)}, s32[256]{0:T(256)}, u32[]{:S(2)}) copy-start(s32[256]{0:T(256)} %param.37) | copy-start | bytes 3076
  17.3 43.1 %copy-start.82 = (bf16[768]{0:T(1024)(128)(2,1)S(1)}, bf16[768]{0:T(1024)(128)(2,1)}, u32[]{:S(2)}) copy-start(bf16[768]{0:T(1024)(128)(2,1)} %param.23) | copy-start | bytes 4612
  17.3 43.1 %copy-start.6 = (bf16[256,768]{1,0:T(8,128)(2,1)S(1)}, bf16[256,768]{1,0:T(8,128)(2,1)}, u32[]{:S(2)}) copy-start(bf16[256,768]{1,0:T(8,128)(2,1)} %param.21) | copy-start | bytes 1179652
  83.6 158.7 %reduce-scatter.3.cloned.1.call-start = ((), (), s32[]{:S(2)}) async-start(), calls=%async_computation.3 | async-start | bytes 3538944 | tf_op jit(solution)/shard_map/reduce_scatter | solution.py:161
  165.6 146.3 %all-gather.5.cloned.1.call-start = ((), (), s32[]{:S(2)}) async-start(), calls=%async_computation.4 | async-start | bytes 3538944 | tf_op jit(solution)/shard_map/all_gather | solution.py:173
  249.4 151.3 %reduce-scatter.5.cloned.1.call-start = ((), (), s32[]{:S(2)}) async-start(), calls=%async_computation.5 | async-start | bytes 3538944 | tf_op jit(solution)/shard_map/reduce_scatter | solution.py:179
  323.9 292.4 %all-reduce.14.cloned.1.call-start = ((), (), s32[]{:S(2)}) async-start(), calls=%async_computation.7 | async-start | bytes 9879552 | tf_op jit(solution)/shard_map/psum | solution.py:14
  430.1 54.4 %copy-start.40 = (f32[768]{0:T(1024)S(1)}, f32[768]{0:T(1024)}, u32[]{:S(2)}) copy-start(f32[768]{0:T(1024)} %get-tuple-element.184) | copy-start | bytes 9220
  430.1 54.4 %copy-start.39 = (f32[768]{0:T(1024)S(1)}, f32[768]{0:T(1024)}, u32[]{:S(2)}) copy-start(f32[768]{0:T(1024)} %get-tuple-element.183) | copy-start | bytes 9220
  430.1 54.5 %copy-start.38 = (f32[768]{0:T(1024)S(1)}, f32[768]{0:T(1024)}, u32[]{:S(2)}) copy-start(f32[768]{0:T(1024)} %get-tuple-element.182) | copy-start | bytes 9220
  430.1 55.8 %copy-start.7 = (bf16[256,768]{1,0:T(8,128)(2,1)S(1)}, bf16[256,768]{1,0:T(8,128)(2,1)}, u32[]{:S(2)}) copy-start(bf16[256,768]{1,0:T(8,128)(2,1)} %param.21) | copy-start | bytes 1179652
  493.7 244.4 %all-reduce.16.cloned.1.call-start = ((), (), s32[]{:S(2)}) async-start(), calls=%async_computation.8 | async-start | bytes 2359296 | tf_op jit(solution)/shard_map/psum | solution.py:201
  501.4 115.1 %copy-start.86 = (bf16[384]{0:T(512)(128)(2,1)S(1)}, bf16[384]{0:T(512)(128)(2,1)}, u32[]{:S(2)}) copy-start(bf16[384]{0:T(512)(128)(2,1)} %get-tuple-element.294) | copy-start | bytes 2308
  501.4 372.6 %all-reduce.12.cloned.1.call-start = ((), (), s32[]{:S(2)}) async-start(), calls=%async_computation.6 | async-start | bytes 9879552 | tf_op jit(solution)/shard_map/psum | solution.py:14
  616.4 126.1 %copy-start.32 = (f32[768]{0:T(1024)S(1)}, f32[768]{0:T(1024)}, u32[]{:S(2)}) copy-start(f32[768]{0:T(1024)} %get-tuple-element.193) | copy-start | bytes 9220
  616.4 126.1 %copy-start.33 = (f32[768]{0:T(1024)S(1)}, f32[768]{0:T(1024)}, u32[]{:S(2)}) copy-start(f32[768]{0:T(1024)} %get-tuple-element.196) | copy-start | bytes 9220
  616.4 126.1 %copy-start.34 = (f32[768]{0:T(1024)S(1)}, f32[768]{0:T(1024)}, u32[]{:S(2)}) copy-start(f32[768]{0:T(1024)} %get-tuple-element.296) | copy-start | bytes 9220
  616.4 126.1 %copy-start.35 = (f32[768]{0:T(1024)S(1)}, f32[768]{0:T(1024)}, u32[]{:S(2)}) copy-start(f32[768]{0:T(1024)} %get-tuple-element.126) | copy-start | bytes 9220
  616.4 126.1 %copy-start.36 = (f32[768]{0:T(1024)S(1)}, f32[768]{0:T(1024)}, u32[]{:S(2)}) copy-start(f32[768]{0:T(1024)} %get-tuple-element.195) | copy-start | bytes 9220
  616.4 126.1 %copy-start.37 = (f32[768]{0:T(1024)S(1)}, f32[768]{0:T(1024)}, u32[]{:S(2)}) copy-start(f32[768]{0:T(1024)} %get-tuple-element.298) | copy-start | bytes 9220
  616.4 217.1 %copy-start.3 = (f32[256,768]{1,0:T(8,128)S(1)}, f32[256,768]{1,0:T(8,128)}, u32[]{:S(2)}) copy-start(f32[256,768]{1,0:T(8,128)} %copy-done.2) | copy-start | bytes 2359300
  616.4 217.1 %copy-start.81 = (f32[256]{0:T(256)S(1)}, f32[256]{0:T(256)}, u32[]{:S(2)}) copy-start(f32[256]{0:T(256)} %copy-done.80) | copy-start | bytes 3076
  (73 other events, 482.8 us)
Sparse Core Ops, SparseCore 0:
  83.7 65.6 all-gather.2
  165.8 76.4 reduce-scatter.2
  249.5 62.4 all-gather.4
  324.1 76.5 reduce-scatter.4
  493.8 122.4 all-reduce.13
  619.9 118.1 all-reduce.15
  740.9 133.0 all-reduce.11
